TPU v7x, 256 devices: a whole 4x4x8 slice. The times are simulated.
256 devices in a mesh: roll: 4 (over z_lo, core), mach: 16 (over y, x), cross: 4 (over z_hi).
Axes of the slice: x: 4, y: 4, z: 8 (z_hi: 4, z_lo: 2; z = z_hi * 2 + z_lo), core: 2. Of those that a mesh axis runs over, the one named last changes fastest.
Arguments:
- density: bfloat16 [128, 4096, 2048], P('roll', 'mach', 'cross'), may hold values from 0 to 1
- roll_start: float32 [32, 128], P(None, 'roll'), may hold values from 0.05 to 1
- mach_factor: bfloat16 [32, 4096], P(None, 'mach'), may hold values from 0.0099487305 to 1
- cross_factor: bfloat16 [32, 2048], P(None, 'cross'), may hold values from 0.0099487305 to 1
Outputs:
- roll_factor: float32 [32, 128], P(None, 'roll')
- mode_two: float32 [32, 4096], P(None, ('mach', 'cross'))
All inputs are finite; a program needn't handle non-finite values.
Results may differ from a plain program's by a relative error of at most 0.0003.
Values sent between devices are 32-bit elements; how exact they have to be, the bound alone decides.
A program may use at most 64 MiB of HBM per device.

v0:
```python
import jax
import jax.numpy as jnp
from jax import lax
from jax.sharding import PartitionSpec as P


def hals_rows(roll_rows, mttkrp, gram):

    def column_step(column, rows):
        column = jnp.asarray(column).astype(jnp.int32)
        gram_row = lax.dynamic_slice_in_dim(gram, column, 1, 0)
        diag_entry = lax.dynamic_slice_in_dim(gram_row, column, 1, 1)
        current = lax.dynamic_slice_in_dim(rows, column, 1, 0)
        target = lax.dynamic_slice_in_dim(mttkrp, column, 1, 0)
        mixed = jnp.dot(gram_row, rows, precision=lax.Precision.HIGHEST)
        updated = jnp.maximum(current + (target - mixed) / diag_entry, 0.0)
        return lax.dynamic_update_slice_in_dim(rows, updated, column, 0)

    return lax.fori_loop(0, roll_rows.shape[0], column_step, roll_rows)


def local(density, roll_start, mach_factor, cross_factor):
    rolls_here, bins_here, cross_here = density.shape
    rank = cross_factor.shape[0]
    flat = density.reshape(rolls_here * bins_here, cross_here)
    partial_value = lax.dot_general(
        cross_factor, flat, (((1,), (1,)), ((), ())), preferred_element_type=jnp.float32
    )
    partial_value = partial_value.reshape(rank, rolls_here, bins_here)
    local_terms = jnp.einsum(
        "rij,rj->ri",
        partial_value,
        mach_factor.astype(jnp.float32),
        precision=lax.Precision.HIGHEST,
    )
    local_mach = jnp.dot(mach_factor, mach_factor.T, preferred_element_type=jnp.float32)
    local_cross = jnp.dot(cross_factor, cross_factor.T, preferred_element_type=jnp.float32)
    a = lax.axis_index("roll")
    m = lax.axis_index("mach")
    c = lax.axis_index("cross")
    nroll = lax.axis_size("roll")
    slots = jnp.zeros((nroll + 2, rank, rank), jnp.float32)
    slots = lax.dynamic_update_slice_in_dim(slots, local_terms[None], a, 0)
    slots = slots.at[nroll].set(jnp.where((a == 0) & (c == 0), local_mach, 0.0))
    slots = slots.at[nroll + 1].set(jnp.where((a == 0) & (m == 0), local_cross, 0.0))
    tot = lax.psum(slots, ("roll", "mach", "cross"))
    mttkrp = lax.dynamic_index_in_dim(tot, a, 0, keepdims=False)
    gram = tot[nroll] * tot[nroll + 1]
    roll_factor = hals_rows(roll_start, mttkrp, gram)
    term = jnp.einsum("rij,ri->rj", partial_value, roll_factor, precision=lax.Precision.HIGHEST)
    nm = lax.axis_size("mach")
    ms = jnp.zeros((nm,) + term.shape, jnp.float32)
    ms = lax.dynamic_update_slice_in_dim(ms, term[None], m, 0)
    whole = lax.psum(ms, ("roll", "mach", "cross"))
    whole = lax.dynamic_index_in_dim(whole, m, 0, keepdims=False)
    span = whole.shape[1] // lax.axis_size("cross")
    total = lax.dynamic_slice_in_dim(whole, c * span, span, 1)
    scale = rank / (rolls_here * nroll * cross_here * lax.axis_size("cross"))
    return (roll_factor, total * scale)


def solution(mesh):
    in_specs = (P("roll", "mach", "cross"), P(None, "roll"), P(None, "mach"), P(None, "cross"))
    out_specs = (P(None, "roll"), P(None, ("mach", "cross")))
    return jax.shard_map(local, mesh=mesh, in_specs=in_specs, out_specs=out_specs, check_vma=False)
```

profile of v0, /device:TPU:2, one launch (start us, length us, event | category | flops | bytes accessed | tf_op | source)
XLA Modules:
  0.0 399.3 jit_solution(10247666444916578830)
XLA Ops:
  7.9 5.9 %fusion.13 = f32[32,32,256]{2,0,1:T(8,128)S(1)} fusion(bf16[32,256,512]{2,1,0:T(8,128)(2,1)} %param.10, bf16[32,512]{1,0:T(8,128)(2,1)S(1)} %copy-done), kind=kOutput, calls=%fused_computation.19 | convolution fusion | flops 268435456 | bytes 9469952 | tf_op jit(solution)/shard_map/dot_general | solution.py:26
  13.8 1.2 fusion.11
  15.3 79.2 %psum.14 = f32[6,32,32]{2,1,0:T(8,128)S(1)} all-reduce(f32[6,32,32]{2,1,0:T(8,128)S(1)} %fusion.6), channel_id=1, replica_groups=mesh['roll'=4,'mach'=16,'cross'=4] {'roll','mach','cross'}, use_global_device_ids=true, to_apply=%region_0.1 | all-reduce | flops 6144 | bytes 49152 | tf_op jit(solution)/shard_map/psum | solution.py:46
  94.5 45.2 %while.18 = (s32[]{:T(128)}, f32[32,32]{1,0:T(8,128)S(1)}, f32[32,32]{1,0:T(8,128)S(1)}, f32[32,32]{1,0:T(8,128)S(1)}, s32[]{:T(128)}, /*index=5*/s32[]{:T(128)}, s32[]{:T(128)}) while((s32[]{:T(128)}, f32[32,32]{1,0:T(8,128)S(1)}, f32[32,32]{1,0:T(8,128)S(1)}, f32[32,32]{1,0:T(8,128)S(1)}, s32[]{:T(128)}, /*index=5*/s32[]{:T(128)}, ...), condition=%wide.region_2.3_spmd, body=%wide.region_1.2_spmd.sunk | while | flops 12419 | bytes 19949 | solution.py:19
  95.1 0.8 fusion.29
  96.5 0.8 fusion.29
  97.9 0.8 fusion.29
  99.3 0.8 fusion.29
  100.8 0.8 fusion.29
  102.2 0.8 fusion.29
  103.6 0.8 fusion.29
  105.0 0.8 fusion.29
  106.4 0.8 fusion.29
  107.8 0.8 fusion.29
  109.2 0.8 fusion.29
  110.6 0.8 fusion.29
  112.1 0.8 fusion.29
  113.5 0.8 fusion.29
  114.9 0.8 fusion.29
  116.3 0.8 fusion.29
  139.7 1.3 fusion.9
  141.0 0.8 copy-done.1
  141.9 249.1 %all-reduce.2.cloned.1.call-done = f32[16,32,256]{2,1,0:T(8,128)} async-done(((f32[16,32,256]{2,1,0:T(8,128)}), f32[16,32,256]{2,1,0:T(8,128)}) %all-reduce.2.cloned.1.call-update) | async-done | bytes 524304 | tf_op jit(solution)/shard_map/psum | solution.py:54
  391.0 1.4 multiply_bitcast_fusion
  (98 shorter events, 33.2 us)
Async XLA Ops:
  7.2 0.8 copy-start
  7.2 6.7 %copy-start.4 = (bf16[32,256]{1,0:T(8,128)(2,1)S(1)}, bf16[32,256]{1,0:T(8,128)(2,1)}, u32[]{:S(2)}) copy-start(bf16[32,256]{1,0:T(8,128)(2,1)} %param.12) | copy-start | bytes 49156
  7.2 87.3 %copy-start.3 = (f32[32,32]{1,0:T(8,128)S(1)}, f32[32,32]{1,0:T(8,128)}, u32[]{:S(2)}) copy-start(f32[32,32]{1,0:T(8,128)} %param.11) | copy-start | bytes 12292
  7.2 383.8 %all-reduce.2.cloned.1.call-start = ((), (), s32[]{:S(2)}) async-start(), calls=%async_computation | async-start | bytes 1048576 | tf_op jit(solution)/shard_map/psum | solution.py:54
  139.7 252.8 %copy-start.2 = (f32[32,32]{1,0:T(8,128)}, f32[32,32]{1,0:T(8,128)S(1)}, u32[]{:S(2)}) copy-start(f32[32,32]{1,0:T(8,128)S(1)} %get-tuple-element.148) | copy-start | bytes 12292
  141.0 0.8 copy-start.1
Sparse Core Ops, SparseCore 0:
  142.0 248.9 all-reduce.1
where the time goes:
time: 400 us; the launch traced here: 399 us
  waiting for transfers between devices  249 us (62%)
  blocking collectives  79.2 us (20%)
  matrix products  33.6 us (8%)
  local copies, waits for them, and re-layouts  21.2 us (5%)
  between operations  14.2 us (4%)
    psum x1, waiting for transfers between devices, local(): whole = lax.psum(ms, ('roll', 'mach', 'cross'))  249 us
    psum x1, blocking collectives, local(): tot = lax.psum(slots, ('roll', 'mach', 'cross'))  79.2 us
    dot_general x32, matrix products, column_step(): mixed = jnp.dot(gram_row, rows, precision=lax.Precision.HIGHEST)  25 us
    dynamic_slice x32, local copies, waits for them, and re-layouts, column_step(): diag_entry = lax.dynamic_slice_in_dim(gram_row, column, 1, 1)  18.8 us
  transfers between devices with their start and end apart: 1, of which 1 were waited for; matrix products, arithmetic and copies ran while one was open for 0% of the time, Pallas kernels for 0%

commit v1 on v0

--- a/solution.py
+++ b/solution.py
@@ -51,7 +51,7 @@
     nm = lax.axis_size("mach")
     ms = jnp.zeros((nm,) + term.shape, jnp.float32)
     ms = lax.dynamic_update_slice_in_dim(ms, term[None], m, 0)
-    whole = lax.psum(ms, ("roll", "mach", "cross"))
+    whole = lax.psum(lax.psum(ms, ("mach", "cross")), "roll")
     whole = lax.dynamic_index_in_dim(whole, m, 0, keepdims=False)
     span = whole.shape[1] // lax.axis_size("cross")
     total = lax.dynamic_slice_in_dim(whole, c * span, span, 1)

time: 400 us -> 921 us (2.30)
  waiting for transfers between devices: 249 us -> 768 us
    psum x1 -> x2, waiting for transfers between devices: 249 us -> 768 us  [local(): whole = lax.psum(lax.psum(ms, ('mach', 'cross')), 'roll')]
  transfers between devices with their start and end apart: 1 -> 2, of which waited for: 1 -> 2; matrix products, arithmetic and copies ran while one was open for 0% -> 0% of each run, Pallas kernels for 0% -> 0%
where the time goes in v1:
time: 921 us; the launch traced here: 919 us
  waiting for transfers between devices  768 us (83%)
  blocking collectives  79.2 us (9%)
  matrix products  33.6 us (4%)
  local copies, waits for them, and re-layouts  21.2 us (2%)
  between operations  14.2 us (2%)
    psum x2, waiting for transfers between devices, local(): whole = lax.psum(lax.psum(ms, ('mach', 'cross')), 'roll')  768 us
    psum x1, blocking collectives, local(): tot = lax.psum(slots, ('roll', 'mach', 'cross'))  79.2 us
    dot_general x32, matrix products, column_step(): mixed = jnp.dot(gram_row, rows, precision=lax.Precision.HIGHEST)  25 us
    dynamic_slice x32, local copies, waits for them, and re-layouts, column_step(): diag_entry = lax.dynamic_slice_in_dim(gram_row, column, 1, 1)  18.8 us
  transfers between devices with their start and end apart: 2, of which 2 were waited for; matrix products, arithmetic and copies ran while one was open for 0% of the time, Pallas kernels for 0%

profile of v1, /device:TPU:2, one launch (start us, length us, event | category | flops | bytes accessed | tf_op | source)
XLA Modules:
  0.0 918.6 jit_solution(9907768711191541369)
XLA Ops:
  7.9 5.9 fusion.13
  13.8 1.2 fusion.11
  15.3 79.2 %psum.21 = f32[6,32,32]{2,1,0:T(8,128)S(1)} all-reduce(f32[6,32,32]{2,1,0:T(8,128)S(1)} %fusion.6), channel_id=1, replica_groups=mesh['roll'=4,'mach'=16,'cross'=4] {'roll','mach','cross'}, use_global_device_ids=true, to_apply=%region_0.1 | all-reduce | flops 6144 | bytes 49152 | tf_op jit(solution)/shard_map/psum | solution.py:46
  94.5 45.2 %while.18 = (s32[]{:T(128)}, f32[32,32]{1,0:T(8,128)S(1)}, f32[32,32]{1,0:T(8,128)S(1)}, f32[32,32]{1,0:T(8,128)S(1)}, s32[]{:T(128)}, /*index=5*/s32[]{:T(128)}, s32[]{:T(128)}) while((s32[]{:T(128)}, f32[32,32]{1,0:T(8,128)S(1)}, f32[32,32]{1,0:T(8,128)S(1)}, f32[32,32]{1,0:T(8,128)S(1)}, s32[]{:T(128)}, /*index=5*/s32[]{:T(128)}, ...), condition=%wide.region_2.3_spmd, body=%wide.region_1.2_spmd.sunk | while | flops 12419 | bytes 19949 | solution.py:19
  95.1 0.8 fusion.29
  96.5 0.8 fusion.29
  97.9 0.8 fusion.29
  99.4 0.8 fusion.29
  100.8 0.8 fusion.29
  102.2 0.8 fusion.29
  103.6 0.8 fusion.29
  106.4 0.8 fusion.29
  107.8 0.8 fusion.29
  109.2 0.8 fusion.29
  110.6 0.8 fusion.29
  112.1 0.8 fusion.29
  113.5 0.8 fusion.29
  114.9 0.8 fusion.29
  116.3 0.8 fusion.29
  139.7 1.3 fusion.9
  141.0 0.8 copy-done.1
  141.9 721.2 %all-reduce.3.cloned.1.call-done = f32[16,32,256]{2,1,0:T(8,128)} async-done(((f32[16,32,256]{2,1,0:T(8,128)}), f32[16,32,256]{2,1,0:T(8,128)}) %all-reduce.3.cloned.1.call-update) | async-done | bytes 524304 | tf_op jit(solution)/shard_map/psum | solution.py:54
  863.1 47.2 %all-reduce.5.cloned.1.call-done = f32[16,32,256]{2,1,0:T(8,128)} async-done(((f32[16,32,256]{2,1,0:T(8,128)}), f32[16,32,256]{2,1,0:T(8,128)}) %all-reduce.5.cloned.1.call-update) | async-done | bytes 524304 | tf_op jit(solution)/shard_map/psum | solution.py:54
  910.3 1.4 multiply_bitcast_fusion
  (101 shorter events, 34.1 us)
Async XLA Ops:
  7.2 0.8 copy-start
  7.2 6.7 copy-start.4
  7.2 87.3 %copy-start.3 = (f32[32,32]{1,0:T(8,128)S(1)}, f32[32,32]{1,0:T(8,128)}, u32[]{:S(2)}) copy-start(f32[32,32]{1,0:T(8,128)} %param.11) | copy-start | bytes 12292
  7.2 855.9 %all-reduce.3.cloned.1.call-start = ((), (), s32[]{:S(2)}) async-start(), calls=%async_computation | async-start | bytes 1048576 | tf_op jit(solution)/shard_map/psum | solution.py:54
  139.7 772.1 %copy-start.2 = (f32[32,32]{1,0:T(8,128)}, f32[32,32]{1,0:T(8,128)S(1)}, u32[]{:S(2)}) copy-start(f32[32,32]{1,0:T(8,128)S(1)} %get-tuple-element.148) | copy-start | bytes 12292
  141.0 0.8 copy-start.1
  141.9 768.4 %all-reduce.5.cloned.1.call-start = ((), (), s32[]{:S(2)}) async-start(), calls=%async_computation.1 | async-start | bytes 1048576 | tf_op jit(solution)/shard_map/psum | solution.py:54
Sparse Core Ops, SparseCore 0:
  142.0 721.0 all-reduce.2
  865.9 44.3 all-reduce.4
